TPU v7x, 32 devices: a whole 2x2x4 slice. The times are simulated.
32 devices in a mesh: win: 4 (over z), seq: 8 (over y, x, core).
Axes of the slice: x: 2, y: 2, z: 4, core: 2. Of those that a mesh axis runs over, the one named last changes fastest.
Arguments:
- layer_input: bfloat16 [8, 1024, 768], P('win', 'seq'), may hold values from -6 to 6
- d_out: bfloat16 [8, 1024, 768], P('win', 'seq'), may hold values from -13.5 to 13.5
- rand_ids: int32 [8, 16, 12, 3], P('win', 'seq'), may hold values from 0 to 15
- live_mask: int32 [8], P('win'), may hold values 0 or 1
- w_qkv: float32 [768, 2304], P('seq', 'win'), may hold values from -0.21875 to 0.21875
- w_out: float32 [768, 768], P('seq', 'win'), may hold values from -0.875 to 0.875
- w_up: float32 [768, 3072], P('seq', 'win'), may hold values from -0.25259074 to 0.25259074
- w_down: float32 [3072, 768], P('seq', 'win'), may hold values from -0.109375 to 0.109375
- norm_params: float32 [3072], P(('win', 'seq')), may hold values from -1.2 to 2, as said below
- m_qkv: float32 [768, 2304], P('seq', 'win'), may hold values from -0.0015031901 to 0.0015031901, as said below
- m_out: float32 [768, 768], P('seq', 'win'), may hold values from -0.0015031901 to 0.0015031901, as said below
- m_up: float32 [768, 3072], P('seq', 'win'), may hold values from -0.0015031901 to 0.0015031901, as said below
- m_down: float32 [3072, 768], P('seq', 'win'), may hold values from -0.0015031901 to 0.0015031901, as said below
- m_norm: float32 [3072], P(('win', 'seq')), may hold values from -0.0060127606 to 0.0060127606, as said below
- v_qkv: float32 [768, 2304], P('seq', 'win'), may hold values from 1.412238e-07 to 5.648952e-07
- v_out: float32 [768, 768], P('seq', 'win'), may hold values from 1.412238e-07 to 5.648952e-07
- v_up: float32 [768, 3072], P('seq', 'win'), may hold values from 1.412238e-07 to 5.648952e-07
- v_down: float32 [3072, 768], P('seq', 'win'), may hold values from 1.412238e-07 to 5.648952e-07
- v_norm: float32 [3072], P(('win', 'seq')), may hold values from 2.2595806e-06 to 9.0383225e-06
Outputs:
- output: bfloat16 [8, 1024, 768], P('win', 'seq')
- d_input: float32 [8, 1024, 768], P('win', 'seq')
- g_qkv: float32 [768, 2304], P('seq', 'win')
- g_out: float32 [768, 768], P('seq', 'win')
- g_up: float32 [768, 3072], P('seq', 'win')
- g_down: float32 [3072, 768], P('seq', 'win')
- g_norm: float32 [3072], P(('win', 'seq'))
- new_qkv: float32 [768, 2304], P('seq', 'win')
- new_out: float32 [768, 768], P('seq', 'win')
- new_up: float32 [768, 3072], P('seq', 'win')
- new_down: float32 [3072, 768], P('seq', 'win')
- new_norm: float32 [3072], P(('win', 'seq'))
- mom_qkv: float32 [768, 2304], P('seq', 'win')
- mom_out: float32 [768, 768], P('seq', 'win')
- mom_up: float32 [768, 3072], P('seq', 'win')
- mom_down: float32 [3072, 768], P('seq', 'win')
- mom_norm: float32 [3072], P(('win', 'seq'))
- sec_qkv: float32 [768, 2304], P('seq', 'win')
- sec_out: float32 [768, 768], P('seq', 'win')
- sec_up: float32 [768, 3072], P('seq', 'win')
- sec_down: float32 [3072, 768], P('seq', 'win')
- sec_norm: float32 [3072], P(('win', 'seq'))
- grad_norm: float32 [1], replicated
Inputs may be any that keep to these rules, and one draw needn't show every extreme that they name: `norm_params`: gains about 1 in the first and third pieces, shifts of both signs in the second and fourth. `m_qkv`: of both signs. `m_out`: of both signs. `m_up`: of both signs. `m_down`: of both signs. `m_norm`: of both signs.
All inputs are finite; a program needn't handle non-finite values. No bound on the sum of `live_mask` on one device may be relied on, other than what follows from the above.
Results may differ from a plain program's by a relative error of at most 0.035.
Values may be sent and summed in bfloat16 or wider, within the bound.
A program may use at most 320 MiB of HBM per device.

v0:
```python
import math
import jax
import jax.numpy as jnp
from jax import lax
from jax.sharding import PartitionSpec as P

H = 12
HD = 64
BLK = 64
STEP = 3
NEG = -1e30
ln_eps = 1e-05
beta_one = 0.5
beta_two = 0.5
adam_eps = 1e-08
decay_rate = 0.1
rate_matrix = 0.04
rate_output = 0.16
rate_norm = 0.6


def layer_norm(values, gain, shift):
    centre = values - jnp.mean(values, axis=-1, keepdims=True)
    spread = jnp.mean(centre * centre, axis=-1, keepdims=True)
    return centre * lax.rsqrt(spread + ln_eps) * gain + shift


def slot_counts(rand_ids, first_block, block_count):
    blocks_dev = rand_ids.shape[1]
    here = (first_block + jnp.arange(blocks_dev, dtype=jnp.int32))[:, None]
    every = jnp.arange(block_count, dtype=jnp.int32)[None, :]
    near = (jnp.abs(here - every) <= 1).astype(jnp.float32)
    ends = (every == 0).astype(jnp.float32) + (every == block_count - 1).astype(jnp.float32)
    drawn = jnp.sum((rand_ids[..., None] == every[0]).astype(jnp.float32), axis=3)
    return (near + ends)[None, :, None, :] + drawn


def adam_update(weight, grad, first, second, rate, decay, fix_one, fix_two):
    first_new = beta_one * first + (1.0 - beta_one) * grad
    second_new = beta_two * second + (1.0 - beta_two) * grad * grad
    stride = first_new / fix_one / (jnp.sqrt(second_new / fix_two) + adam_eps)
    return (weight - rate * (stride + decay * weight), first_new, second_new)


def per_device(
    layer_input,
    d_out,
    rand_ids,
    live_mask,
    w_qkv,
    w_out,
    w_up,
    w_down,
    norm_params,
    m_qkv,
    m_out,
    m_up,
    m_down,
    m_norm,
    v_qkv,
    v_out,
    v_up,
    v_down,
    v_norm,
):
    wins, local_len, width = layer_input.shape
    blocks_dev = local_len // BLK
    block_count = blocks_dev * lax.axis_size("seq")
    first_block = lax.axis_index("seq") * blocks_dev
    inv_root = 1.0 / math.sqrt(HD)
    rows = wins * local_len
    low_qkv = w_qkv.astype(jnp.bfloat16)
    low_out = w_out.astype(jnp.bfloat16)
    low_up = w_up.astype(jnp.bfloat16)
    low_down = w_down.astype(jnp.bfloat16)
    low_norm = norm_params.astype(jnp.bfloat16)
    full_qkv, full_out, full_up, full_down = (
        lax.all_gather(lax.all_gather(low, "win", axis=1, tiled=True), "seq", axis=0, tiled=True)
        for low in (low_qkv, low_out, low_up, low_down)
    )
    full_norm = lax.all_gather(low_norm, ("win", "seq"), axis=0, tiled=True)
    gains = full_norm.astype(jnp.float32).reshape(4, width)
    loss_weight = live_mask.astype(jnp.float32)
    counts = slot_counts(rand_ids, first_block, block_count)
    bias = jnp.where(counts > 0, jnp.log(jnp.maximum(counts, 1.0)), NEG)
    bias = jnp.repeat(bias, BLK, axis=3)[:, :, :, None, :]
    tokens = layer_input.astype(jnp.float32).reshape(rows, width)
    h_one = layer_norm(tokens, gains[0], gains[1]).astype(jnp.bfloat16)
    qkv = jnp.dot(h_one, full_qkv, preferred_element_type=jnp.float32)
    q_heads = qkv[:, :width].astype(jnp.bfloat16).reshape(wins, blocks_dev, BLK, H, HD)
    keyval = qkv[:, width:].astype(jnp.bfloat16).reshape(wins, local_len, 2 * width)
    window = lax.all_gather(keyval, "seq", axis=1, tiled=True)
    shaped = window.reshape(wins, block_count * BLK, 2, H, HD)
    keys, values = (shaped[:, :, 0], shaped[:, :, 1])
    scores = (
        jnp.einsum("wbqhd,wkhd->wbhqk", q_heads, keys, preferred_element_type=jnp.float32)
        * inv_root
        + bias
    )
    top = jnp.max(scores, axis=-1, keepdims=True)
    log_total = top + jnp.log(jnp.sum(jnp.exp(scores - top), axis=-1, keepdims=True))
    prob = jnp.exp(scores - log_total).astype(jnp.bfloat16)
    heads_out = jnp.einsum("wbhqk,wkhd->wbqhd", prob, values, preferred_element_type=jnp.float32)
    attended = heads_out.astype(jnp.bfloat16).reshape(rows, width)
    middle = tokens + jnp.dot(attended, full_out, preferred_element_type=jnp.float32)
    h_two = layer_norm(middle, gains[2], gains[3]).astype(jnp.bfloat16)
    up_proj = jnp.dot(h_two, full_up, preferred_element_type=jnp.float32)
    active = jax.nn.gelu(up_proj).astype(jnp.bfloat16)
    result = middle + jnp.dot(active, full_down, preferred_element_type=jnp.float32)
    output = result.astype(jnp.bfloat16).reshape(wins, local_len, width)
    grad_y = (d_out.astype(jnp.float32) * loss_weight[:, None, None]).reshape(rows, width)
    grad_ffn = grad_y.astype(jnp.bfloat16)
    raw_down = jnp.einsum("tf,td->fd", active, grad_ffn, preferred_element_type=jnp.float32)
    grad_act = jnp.einsum("td,fd->tf", grad_ffn, full_down, preferred_element_type=jnp.float32)
    gelu_pull = jax.vjp(jax.nn.gelu, up_proj)[1]
    grad_up = gelu_pull(grad_act)[0].astype(jnp.bfloat16)
    raw_up = jnp.einsum("td,tf->df", h_two, grad_up, preferred_element_type=jnp.float32)
    grad_h_two = jnp.einsum("tf,df->td", grad_up, full_up, preferred_element_type=jnp.float32)
    norm_pull = jax.vjp(layer_norm, middle, gains[2], gains[3])[1]
    grad_mid_ln, raw_gain_two, raw_shift_two = norm_pull(grad_h_two)
    grad_mid = grad_y + grad_mid_ln
    grad_att = grad_mid.astype(jnp.bfloat16)
    raw_out = jnp.einsum("td,te->de", attended, grad_att, preferred_element_type=jnp.float32)
    grad_o = jnp.einsum("te,de->td", grad_att, full_out, preferred_element_type=jnp.float32)
    grad_o = grad_o.astype(jnp.bfloat16).reshape(wins, blocks_dev, BLK, H, HD)
    grad_p = jnp.einsum("wbqhd,wkhd->wbhqk", grad_o, values, preferred_element_type=jnp.float32)
    prob_f = prob.astype(jnp.float32)
    inner = jnp.sum(prob_f * grad_p, axis=-1, keepdims=True)
    grad_s = (prob_f * (grad_p - inner)).astype(jnp.bfloat16)
    grad_q = (
        jnp.einsum("wbhqk,wkhd->wbqhd", grad_s, keys, preferred_element_type=jnp.float32) * inv_root
    )
    grad_v = jnp.einsum("wbhqk,wbqhd->wkhd", prob, grad_o, preferred_element_type=jnp.float32)
    grad_k = (
        jnp.einsum("wbhqk,wbqhd->wkhd", grad_s, q_heads, preferred_element_type=jnp.float32)
        * inv_root
    )
    grad_kv = jnp.stack([grad_k, grad_v], axis=2).astype(jnp.bfloat16)
    grad_kv = lax.psum_scatter(
        grad_kv.reshape(wins, block_count * BLK, 2 * width), "seq", scatter_dimension=1, tiled=True
    ).reshape(rows, 2 * width)
    grad_qkv = jnp.concatenate([grad_q.reshape(rows, width).astype(jnp.bfloat16), grad_kv], axis=1)
    raw_qkv = jnp.einsum("td,te->de", h_one, grad_qkv, preferred_element_type=jnp.float32)
    grad_h_one = jnp.einsum("te,de->td", grad_qkv, full_qkv, preferred_element_type=jnp.float32)
    first_pull = jax.vjp(layer_norm, tokens, gains[0], gains[1])[1]
    grad_tok_ln, raw_gain_one, raw_shift_one = first_pull(grad_h_one)
    d_input = (grad_mid + grad_tok_ln).reshape(wins, local_len, width)
    raw_norm = jnp.concatenate([raw_gain_one, raw_shift_one, raw_gain_two, raw_shift_two])
    red_qkv, red_out, red_up, red_down = (
        lax.psum_scatter(
            lax.psum_scatter(raw.astype(jnp.bfloat16), "seq", scatter_dimension=0, tiled=True),
            "win",
            scatter_dimension=1,
            tiled=True,
        ).astype(jnp.float32)
        for raw in (raw_qkv, raw_out, raw_up, raw_down)
    )
    red_norm = lax.psum_scatter(raw_norm, ("win", "seq"), scatter_dimension=0, tiled=True)
    reduced = (red_qkv, red_out, red_up, red_down, red_norm)
    local_squares = jnp.float32(0.0)
    for grad in reduced:
        local_squares = local_squares + jnp.sum(grad * grad)
    grad_norm = jnp.sqrt(lax.psum(local_squares, ("win", "seq")))
    factor = 1.0 / jnp.maximum(grad_norm, 1.0)
    clipped = tuple((grad * factor for grad in reduced))
    count = jnp.float32(STEP)
    fix_one = 1.0 - jnp.power(jnp.float32(beta_one), count)
    fix_two = 1.0 - jnp.power(jnp.float32(beta_two), count)
    params = (w_qkv, w_out, w_up, w_down, norm_params)
    firsts = (m_qkv, m_out, m_up, m_down, m_norm)
    seconds = (v_qkv, v_out, v_up, v_down, v_norm)
    rates = (rate_matrix, rate_output, rate_matrix, rate_matrix, rate_norm)
    news, moms, secs = ([], [], [])
    for index in range(5):
        decay = 0.0 if index == 4 else decay_rate
        new_w, new_m, new_v = adam_update(
            params[index],
            clipped[index],
            firsts[index],
            seconds[index],
            rates[index],
            decay,
            fix_one,
            fix_two,
        )
        news.append(new_w)
        moms.append(new_m)
        secs.append(new_v)
    return (
        output,
        d_input,
        clipped[0],
        clipped[1],
        clipped[2],
        clipped[3],
        clipped[4],
        news[0],
        news[1],
        news[2],
        news[3],
        news[4],
        moms[0],
        moms[1],
        moms[2],
        moms[3],
        moms[4],
        secs[0],
        secs[1],
        secs[2],
        secs[3],
        secs[4],
        grad_norm.reshape(1),
    )


def solution(mesh):
    placed = (
        P("win", "seq", None),
        P("win", "seq", None),
        P("win", "seq", None, None),
        P("win"),
        P("seq", "win"),
        P("seq", "win"),
        P("seq", "win"),
        P("seq", "win"),
        P(("win", "seq")),
        P("seq", "win"),
        P("seq", "win"),
        P("seq", "win"),
        P("seq", "win"),
        P(("win", "seq")),
        P("seq", "win"),
        P("seq", "win"),
        P("seq", "win"),
        P("seq", "win"),
        P(("win", "seq")),
    )
    return jax.shard_map(
        per_device,
        mesh=mesh,
        in_specs=placed,
        out_specs=(
            P("win", "seq", None),
            P("win", "seq", None),
            P("seq", "win"),
            P("seq", "win"),
            P("seq", "win"),
            P("seq", "win"),
            P(("win", "seq")),
            P("seq", "win"),
            P("seq", "win"),
            P("seq", "win"),
            P("seq", "win"),
            P(("win", "seq")),
            P("seq", "win"),
            P("seq", "win"),
            P("seq", "win"),
            P("seq", "win"),
            P(("win", "seq")),
            P("seq", "win"),
            P("seq", "win"),
            P("seq", "win"),
            P("seq", "win"),
            P(("win", "seq")),
            P(),
        ),
        check_vma=False,
    )
```

profile of v0, /device:TPU:0, one launch (start us, length us, event | category | flops | bytes accessed | tf_op | source)
XLA Modules:
  0.0 680.8 jit_solution(3838037226972411840)
XLA Ops:
  8.3 17.0 %all-gather = bf16[4,576,96]{1,2,0:T(8,128)(2,1)S(1)} all-gather(bf16[1,576,96]{1,2,0:T(8,128)(2,1)S(1)} %convert_bitcast_fusion), channel_id=1, replica_groups=mesh['win'=4,'seq'=8] {'win'}, dimensions={0}, use_global_device_ids=true | all-gather | bytes 552960 | tf_op jit(solution)/shard_map/all_gather | solution.py:78
  26.8 17.4 %all_gather.38 = bf16[384,768]{0,1:T(8,128)(2,1)} all-gather(bf16[384,192]{0,1:T(8,128)(2,1)S(1)} %convert_element_type.148), channel_id=1, replica_groups=mesh['win'=4,'seq'=8] {'win'}, dimensions={1}, use_global_device_ids=true | all-gather | bytes 737280 | tf_op jit(solution)/shard_map/all_gather | solution.py:78
  44.6 39.8 %all-reduce = bf16[3072]{0:T(1024)(128)(2,1)S(1)} all-reduce(bf16[3072]{0:T(1024)(128)(2,1)S(1)} %dynamic-update-slice), channel_id=1, replica_groups=mesh['win'=4,'seq'=8] {'win','seq'}, use_global_device_ids=true, to_apply=%add | all-reduce | flops 3072 | bytes 12288
  85.7 3.1 convolution_convert_fusion.3
  90.3 14.1 %all_gather.34 = bf16[96,768]{0,1:T(8,128)(2,1)S(1)} all-gather(bf16[96,192]{0,1:T(8,128)(2,1)S(1)} %copy.161), channel_id=1, replica_groups=mesh['win'=4,'seq'=8] {'win'}, dimensions={1}, use_global_device_ids=true | all-gather | bytes 184320 | tf_op jit(solution)/shard_map/all_gather | solution.py:78
  105.3 16.1 %all_gather.36 = bf16[96,3072]{1,0:T(8,128)(2,1)} all-gather(bf16[96,768]{1,0:T(8,128)(2,1)S(1)} %convert_element_type.146), channel_id=1, replica_groups=mesh['win'=4,'seq'=8] {'win'}, dimensions={1}, use_global_device_ids=true | all-gather | bytes 737280 | tf_op jit(solution)/shard_map/all_gather | solution.py:78
  125.2 5.4 fusion.66
  130.6 23.8 %all-gather.9.cloned.1.call-done = bf16[2,1024,1536]{1,2,0:T(8,128)(2,1)} async-done(((bf16[2,128,1536]{1,2,0:T(8,128)(2,1)}), bf16[2,1024,1536]{1,2,0:T(8,128)(2,1)}) %all-gather.9.cloned.1.call-update) | async-done | bytes 6291472 | tf_op jit(solution)/shard_map/all_gather | solution.py:92
  154.4 3.7 fusion.17
  159.3 3.2 exponential_reduce_fusion
  162.6 2.4 exponential_convert_fusion
  165.0 7.3 %fusion.30 = bf16[2,2,64,12,64]{2,4,1,3,0:T(8,128)(2,1)S(1)} fusion(bf16[2,2,12,64,1024]{4,3,1,2,0:T(8,128)(2,1)S(1)} %exponential_convert_fusion, bf16[2,1024,2,12,64]{1,4,3,2,0:T(8,128)(2,1)} %bitcast.173), kind=kOutput, calls=%fused_computation.43 | convolution fusion | flops 402849792 | bytes 9830400 | tf_op jit(solution)/shard_map/wbhqk,wkhd->wbqhd/dot_general | solution.py:103
  173.6 7.1 %all-gather.11.cloned.1.call-done = bf16[768,768]{1,0:T(8,128)(2,1)} async-done(((bf16[96,768]{1,0:T(8,128)(2,1)}), bf16[768,768]{1,0:T(8,128)(2,1)}) %all-gather.11.cloned.1.call-update) | async-done | bytes 1179664 | tf_op jit(solution)/shard_map/all_gather | solution.py:78
  180.8 1.8 fusion.65
  182.9 38.6 %all-gather.13.cloned.1.call-done = bf16[768,3072]{1,0:T(8,128)(2,1)} async-done(((bf16[96,3072]{1,0:T(8,128)(2,1)}), bf16[768,3072]{1,0:T(8,128)(2,1)}) %all-gather.13.cloned.1.call-update) | async-done | bytes 4718608 | tf_op jit(solution)/shard_map/all_gather | solution.py:78
  221.4 7.8 %fusion.10 = (bf16[256,3072]{1,0:T(8,128)(2,1)S(1)}, f32[256,3072]{1,0:T(8,128)}) fusion(f32[256,3072]{1,0:T(8,128)} %fusion.66, bf16[768,3072]{1,0:T(8,128)(2,1)} %all-gather.13.cloned.1.call-done, f32[256,768]{1,0:T(8,128)S(1)} %get-tuple-element.196, f32[768]{0:T(1024)S(1)} %get-tuple-element.190, f32[768]{0:T(1024)S(1)} %get-tuple-element.189, ...), kind=kOutput, calls=%fused_computation.24 | convolution fusion | flops 1224671232 | bytes 13377536 | tf_op jit(solution)/shard_map/dot_general | solution.py:107
  232.9 6.3 convolution_convert_fusion
  239.3 5.2 convolution_convert_fusion.1
  245.0 1.8 convolution_convert_fusion.5
  250.0 5.7 fusion.12
  255.7 6.3 fusion.13
  261.9 7.8 %fusion = f32[2,2,12,64]{3,1,2,0:T(2,128)S(1)} fusion(f32[2,2,12,64,1024]{4,3,1,2,0:T(8,128)} %bitcast.165, bf16[2,2,12,64,1024]{4,3,1,2,0:T(8,128)(2,1)} %copy-done.1), kind=kLoop, calls=%fused_computation.2 | loop fusion | flops 9434112 | bytes 18886656 | tf_op jit(solution)/shard_map/reduce_sum | solution.py:128
  269.7 9.6 %fusion.1 = bf16[2,2,12,64,1024]{4,3,1,2,0:T(8,128)(2,1)S(1)} fusion(f32[2,2,12,64]{3,1,2,0:T(2,128)S(1)} %fusion, f32[2,12,1024,128]{2,3,1,0} %fusion.13, f32[2,2,12,64]{3,1,2,0:T(2,128)S(1)} %bitcast.188, f32[2,2,12,1024]{3,1,2,0:T(2,128)S(1)} %copy-done.8, f32[2,12,1024,128]{2,3,1,0} %copy-done), kind=kLoop, calls=%fused_computation.3 | loop fusion | flops 25165824 | bytes 31678464 | tf_op jit(solution)/shard_map/convert_element_type | solution.py:129
  279.4 2.7 copy-done.2
  284.9 3.4 copy.168
  288.3 16.6 %copy.184 = bf16[2,1024,1536]{2,0,1:T(2,128)(2,1)} copy(bf16[2,1024,1536]{1,2,0:T(8,128)(2,1)} %bitcast.167) | data formatting | bytes 12582912
  304.9 7.2 %copy.200 = bf16[128,8,2,1536]{3,1,2,0:T(8,128)(2,1)} copy(bf16[128,8,2,1536]{3,2,1,0:T(2,128)(2,1)} %bitcast.168) | data formatting | bytes 12582912
  312.1 1.7 copy.188
  313.9 13.7 %reduce-scatter.26.cloned.1.call-done = bf16[384,768]{1,0:T(8,128)(2,1)} async-done(((bf16[3072,768]{1,0:T(8,128)(2,1)}), bf16[384,768]{1,0:T(8,128)(2,1)}) %reduce-scatter.26.cloned.1.call-update) | async-done | bytes 589840 | tf_op jit(solution)/shard_map/reduce_scatter | solution.py:151
  327.6 2.1 copy.190
  329.8 55.2 %reduce-scatter.22.cloned.1.call-done = bf16[96,3072]{1,0:T(8,128)(2,1)} async-done(((bf16[768,3072]{1,0:T(8,128)(2,1)}), bf16[96,3072]{1,0:T(8,128)(2,1)}) %reduce-scatter.22.cloned.1.call-update) | async-done | bytes 589840 | tf_op jit(solution)/shard_map/reduce_scatter | solution.py:151
  385.2 6.9 %fusion.33 = bf16[2,2,64,12,64]{2,4,1,3,0:T(8,128)(2,1)S(1)} fusion(bf16[2,2,12,64,1024]{4,3,1,2,0:T(8,128)(2,1)} %copy-done.2, bf16[2,1024,2,12,64]{1,4,3,2,0:T(8,128)(2,1)} %bitcast.174), kind=kOutput, calls=%fused_computation.44 | convolution fusion | flops 403046400 | bytes 9830400 | tf_op jit(solution)/shard_map/wbhqk,wkhd->wbqhd/dot_general | solution.py:131
  393.7 2.6 reshape.263
  396.3 54.2 %reduce-scatter.28.cloned.1.call-done = bf16[128,3072]{1,0:T(8,128)(2,1)} async-done(((bf16[1024,3072]{1,0:T(8,128)(2,1)}), bf16[128,3072]{1,0:T(8,128)(2,1)}) %reduce-scatter.28.cloned.1.call-update) | async-done | bytes 786448
  450.5 3.2 reshape.265
  455.0 3.9 convolution_convert_fusion.2
  460.1 1.9 copy.171
  462.0 1.9 copy.172
  463.8 6.1 fusion.36
  469.9 2.6 reduce-scatter.32.cloned.1.call-done
  474.1 21.1 %reduce-scatter.34.cloned.1.call-done = bf16[192,384]{1,0:T(8,128)(2,1)} async-done(((bf16[768,384]{1,0:T(8,128)(2,1)}), bf16[192,384]{1,0:T(8,128)(2,1)}) %reduce-scatter.34.cloned.1.call-update) | async-done | bytes 147472
  496.2 21.6 %reduce-scatter.24.cloned.1.call-done = bf16[96,768]{1,0:T(8,128)(2,1)} async-done(((bf16[96,3072]{1,0:T(8,128)(2,1)}), bf16[96,768]{1,0:T(8,128)(2,1)}) %reduce-scatter.24.cloned.1.call-update) | async-done | bytes 147472 | tf_op jit(solution)/shard_map/reduce_scatter | solution.py:150
  520.0 48.1 %reduce-scatter.18.cloned.1.call-done = bf16[96,2304]{1,0:T(8,128)(2,1)} async-done(((bf16[768,2304]{1,0:T(8,128)(2,1)}), bf16[96,2304]{1,0:T(8,128)(2,1)}) %reduce-scatter.18.cloned.1.call-update) | async-done | bytes 442384 | tf_op jit(solution)/shard_map/reduce_scatter | solution.py:151
  568.1 2.1 copy.186
  570.2 3.3 multiply_reduce_fusion.2
  574.1 39.5 %all-reduce.1 = f32[3072]{0:T(1024)S(1)} all-reduce(f32[3072]{0:T(1024)S(1)} %pad_maximum_fusion.4), channel_id=11, replica_groups=mesh['win'=4,'seq'=8] {'win','seq'}, use_global_device_ids=true, to_apply=%region_29.30.clone | all-reduce | flops 3072 | bytes 24576
  622.0 40.8 %psum.7 = f32[]{:T(128)} all-reduce(f32[]{:T(128)S(6)} %add.254), channel_id=1, replica_groups=mesh['win'=4,'seq'=8] {'win','seq'}, use_global_device_ids=true, to_apply=%region_31.32 | all-reduce | flops 1 | bytes 8 | tf_op jit(solution)/shard_map/psum | solution.py:163
  669.8 2.1 multiply_subtract_fusion.2
  (173 shorter events, 45.4 us)
Async XLA Ops:
  7.2 19.6 %copy-start.16 = (f32[384,192]{0,1:T(8,128)S(1)}, f32[384,192]{0,1:T(8,128)}, u32[]{:S(2)}) copy-start(f32[384,192]{0,1:T(8,128)} %param.26) | copy-start | bytes 884740
  7.2 37.1 %copy-start.27 = (f32[96]{0:T(128)S(1)}, f32[96]{0:T(128)}, u32[]{:S(2)}) copy-start(f32[96]{0:T(128)} %param.27) | copy-start | bytes 1156
  7.2 77.1 %copy-start.3 = (bf16[2,128,768]{2,1,0:T(8,128)(2,1)S(1)}, bf16[2,128,768]{2,1,0:T(8,128)(2,1)}, u32[]{:S(2)}) copy-start(bf16[2,128,768]{2,1,0:T(8,128)(2,1)} %param.19) | copy-start | bytes 1179652
  7.2 77.8 %all-gather.7.cloned.1.call-start = ((), (), s32[]{:S(2)}) async-start(), calls=%async_computation.9 | async-start | bytes 3981312 | tf_op jit(solution)/shard_map/all_gather | solution.py:78
  26.7 98.3 %all-gather.15.cloned.1.call-start = ((), (), s32[]{:S(2)}) async-start(), calls=%async_computation.13 | async-start | bytes 5308416 | tf_op jit(solution)/shard_map/all_gather | solution.py:78
  44.2 110.2 %all-gather.9.cloned.1.call-start = ((), (), s32[]{:S(2)}) async-start(), calls=%async_computation.10 | async-start | bytes 7077888 | tf_op jit(solution)/shard_map/all_gather | solution.py:92
  85.0 0.8 copy-start.9
  88.8 1.4 copy-start.20
  88.8 16.4 %copy-start.14 = (f32[96,768]{1,0:T(8,128)S(1)}, f32[96,768]{1,0:T(8,128)}, u32[]{:S(2)}) copy-start(f32[96,768]{1,0:T(8,128)} %param.25) | copy-start | bytes 884740
  88.9 32.6 %copy-start.31 = (s32[2]{0:T(128)S(1)}, s32[2]{0:T(128)}, u32[]{:S(2)}) copy-start(s32[2]{0:T(128)} %param.22) | copy-start | bytes 28
  88.9 32.7 %copy-start.26 = (s32[2,2,12,3]{2,1,3,0:T(2,128)S(1)}, s32[2,2,12,3]{2,1,3,0:T(2,128)}, u32[]{:S(2)}) copy-start(s32[2,2,12,3]{2,1,3,0:T(2,128)} %param.21) | copy-start | bytes 1732
  88.9 33.4 %copy-start.22 = (bf16[2,128,768]{2,1,0:T(8,128)(2,1)S(1)}, bf16[2,128,768]{2,1,0:T(8,128)(2,1)}, u32[]{:S(2)}) copy-start(bf16[2,128,768]{2,1,0:T(8,128)(2,1)} %param.20) | copy-start | bytes 1179652
  90.1 90.6 %all-gather.11.cloned.1.call-start = ((), (), s32[]{:S(2)}) async-start(), calls=%async_computation.11 | async-start | bytes 1327104 | tf_op jit(solution)/shard_map/all_gather | solution.py:78
  105.2 116.3 %all-gather.13.cloned.1.call-start = ((), (), s32[]{:S(2)}) async-start(), calls=%async_computation.12 | async-start | bytes 5308416 | tf_op jit(solution)/shard_map/all_gather | solution.py:78
  121.5 190.7 %reduce-scatter.20.cloned.1.call-start = ((), (), s32[]{:S(2)}) async-start(), calls=%async_computation.15 | async-start | bytes 1327104 | tf_op jit(solution)/shard_map/reduce_scatter | solution.py:151
  122.3 40.2 %copy-start.7 = (f32[2,2,12,1024]{3,1,2,0:T(2,128)}, f32[2,2,12,1024]{3,1,2,0:T(2,128)S(1)}, u32[]{:S(2)}) copy-start(f32[2,2,12,1024]{3,1,2,0:T(2,128)S(1)} %add.238) | copy-start | bytes 589828
  122.5 0.9 copy-start.5
  124.2 1.0 copy-start.23
  158.0 4.6 copy-start
  165.0 7.3 %copy-start.1 = (bf16[2,2,12,64,1024]{4,3,1,2,0:T(8,128)(2,1)}, bf16[2,2,12,64,1024]{4,3,1,2,0:T(8,128)(2,1)S(1)}, u32[]{:S(2)}) copy-start(bf16[2,2,12,64,1024]{4,3,1,2,0:T(8,128)(2,1)S(1)} %exponential_convert_fusion) | copy-start | bytes 18874372
  221.4 7.8 %copy-start.30 = (bf16[768,3072]{1,0:T(8,128)(2,1)S(1)}, bf16[768,3072]{1,0:T(8,128)(2,1)}, u32[]{:S(2)}) copy-start(bf16[768,3072]{1,0:T(8,128)(2,1)} %all-gather.13.cloned.1.call-done) | copy-start | bytes 14155780
  229.2 1.6 copy-start.13
  229.2 2.0 copy-start.6
  232.9 94.7 %reduce-scatter.26.cloned.1.call-start = ((), (), s32[]{:S(2)}) async-start(), calls=%async_computation.18 | async-start | bytes 5308416 | tf_op jit(solution)/shard_map/reduce_scatter | solution.py:151
  239.2 145.7 %reduce-scatter.22.cloned.1.call-start = ((), (), s32[]{:S(2)}) async-start(), calls=%async_computation.16 | async-start | bytes 5308416 | tf_op jit(solution)/shard_map/reduce_scatter | solution.py:151
  244.5 206.0 %reduce-scatter.28.cloned.1.call-start = ((), (), s32[]{:S(2)}) async-start(), calls=%async_computation.19 | async-start | bytes 7077888
  248.4 7.3 %slice-start = ((s8[6291456]{0:T(1024)(128)(4,1)}), s8[4194304]{0:T(1024)(128)(4,1)S(1)}, s32[]{:S(2)}) async-start(s8[6291456]{0:T(1024)(128)(4,1)} %bitcast.175), calls=%async_computation.23 | async-start | bytes 8388608
  249.9 5.7 slice-start.1
  261.9 7.8 %copy-start.8 = (f32[2,2,12,1024]{3,1,2,0:T(2,128)S(1)}, f32[2,2,12,1024]{3,1,2,0:T(2,128)}, u32[]{:S(2)}) copy-start(f32[2,2,12,1024]{3,1,2,0:T(2,128)} %copy-done.7) | copy-start | bytes 589828
  279.4 2.7 copy-start.2
  282.1 2.2 copy-start.4
  312.1 160.5 %reduce-scatter.32.cloned.1.call-start = ((), (), s32[]{:S(2)}) async-start(), calls=%async_computation.21 | async-start | bytes 245760
  313.9 181.2 %reduce-scatter.34.cloned.1.call-start = ((), (), s32[]{:S(2)}) async-start(), calls=%async_computation.22 | async-start | bytes 737280
  329.8 188.0 %reduce-scatter.24.cloned.1.call-start = ((), (), s32[]{:S(2)}) async-start(), calls=%async_computation.17 | async-start | bytes 737280 | tf_op jit(solution)/shard_map/reduce_scatter | solution.py:150
  385.0 183.2 %reduce-scatter.18.cloned.1.call-start = ((), (), s32[]{:S(2)}) async-start(), calls=%async_computation.14 | async-start | bytes 3981312 | tf_op jit(solution)/shard_map/reduce_scatter | solution.py:151
  392.1 62.9 %copy-start.10 = (bf16[256,768]{1,0:T(8,128)(2,1)S(1)}, bf16[256,768]{1,0:T(8,128)(2,1)}, u32[]{:S(2)}) copy-start(bf16[256,768]{1,0:T(8,128)(2,1)} %copy-done.9) | copy-start | bytes 1179652
  458.9 155.4 %reduce-scatter.30.cloned.1.call-start = ((), (), s32[]{:S(2)}) async-start(), calls=%async_computation.20 | async-start | bytes 737280
  573.6 90.0 %copy-start.11 = (f32[384,192]{1,0:T(8,128)S(1)}, f32[384,192]{1,0:T(8,128)}, u32[]{:S(2)}) copy-start(f32[384,192]{1,0:T(8,128)} %copy.171) | copy-start | bytes 884740
  573.6 90.0 %copy-start.12 = (f32[384,192]{1,0:T(8,128)S(1)}, f32[384,192]{1,0:T(8,128)}, u32[]{:S(2)}) copy-start(f32[384,192]{1,0:T(8,128)} %copy.172) | copy-start | bytes 884740
  622.0 45.5 %copy-start.28 = (f32[96]{0:T(128)S(1)}, f32[96]{0:T(128)}, u32[]{:S(2)}) copy-start(f32[96]{0:T(128)} %param.37) | copy-start | bytes 1156
  622.0 45.5 %copy-start.29 = (f32[96]{0:T(128)S(1)}, f32[96]{0:T(128)}, u32[]{:S(2)}) copy-start(f32[96]{0:T(128)} %param.32) | copy-start | bytes 1156
  622.0 46.1 %copy-start.21 = (f32[96,192]{1,0:T(8,128)S(1)}, f32[96,192]{1,0:T(8,128)}, u32[]{:S(2)}) copy-start(f32[96,192]{1,0:T(8,128)} %param.24) | copy-start | bytes 221188
  663.6 6.2 copy-start.17
  663.6 6.2 copy-start.18
  663.9 7.9 %copy-start.15 = (f32[96,768]{1,0:T(8,128)S(1)}, f32[96,768]{1,0:T(8,128)}, u32[]{:S(2)}) copy-start(f32[96,768]{1,0:T(8,128)} %param.25) | copy-start | bytes 884740
  663.9 7.9 %copy-start.19 = (bf16[96,768]{1,0:T(8,128)(2,1)S(1)}, bf16[96,768]{1,0:T(8,128)(2,1)}, u32[]{:S(2)}) copy-start(bf16[96,768]{1,0:T(8,128)(2,1)} %reduce-scatter.24.cloned.1.call-done) | copy-start | bytes 442372
  664.0 7.9 %copy-start.24 = (f32[96,768]{1,0:T(8,128)S(1)}, f32[96,768]{1,0:T(8,128)}, u32[]{:S(2)}) copy-start(f32[96,768]{1,0:T(8,128)} %param.35) | copy-start | bytes 884740
  664.0 7.9 %copy-start.25 = (f32[96,768]{1,0:T(8,128)S(1)}, f32[96,768]{1,0:T(8,128)}, u32[]{:S(2)}) copy-start(f32[96,768]{1,0:T(8,128)} %param.30) | copy-start | bytes 884740
Sparse Core Ops, SparseCore 0:
  26.8 36.0 all-gather.6
  64.8 40.3 all-gather.14
  107.7 46.6 all-gather.8
  156.7 24.0 all-gather.10
  182.5 38.9 all-gather.12
  233.0 36.7 reduce-scatter.19
  273.7 53.8 reduce-scatter.25
  331.1 53.8 reduce-scatter.21
  388.7 61.7 reduce-scatter.27
  453.2 19.3 reduce-scatter.31
  474.9 20.1 reduce-scatter.33
  497.4 20.3 reduce-scatter.23
  521.6 46.4 reduce-scatter.17
  571.0 21.9 reduce-scatter.29
where the time goes:
time: 690 us; the launch traced here: 681 us
  waiting for transfers between devices  286 us (41%)
  blocking collectives  185 us (27%)
  matrix products  78.7 us (11%)
  local copies, waits for them, and re-layouts  69 us (10%)
  other arithmetic  41.1 us (6%)
  between operations  19.9 us (3%)
    reduce_scatter x4, waiting for transfers between devices, per_device(): lax.psum_scatter(raw.astype(jnp.bfloat16), 'seq', scatter_dimension=0, ti...  117 us
    unnamed x2, blocking collectives  79.3 us
    unnamed x18, waiting for transfers between devices  78.1 us
    all_gather x4, blocking collectives, per_device(): lax.all_gather(low, 'win', axis=1, tiled=True)  64.6 us
    unnamed x89, local copies, waits for them, and re-layouts  52.3 us
    all_gather x4, waiting for transfers between devices, per_device(): lax.all_gather(lax.all_gather(low, 'win', axis=1, tiled=True), 'seq', axi...  45.8 us
    psum x1, blocking collectives, per_device(): grad_norm = jnp.sqrt(lax.psum(local_squares, ('win', 'seq')))  40.8 us
    all_gather x1, waiting for transfers between devices, per_device(): window = lax.all_gather(keyval, 'seq', axis=1, tiled=True)  23.8 us
  transfers between devices with their start and end apart: 14, of which 10 were waited for; matrix products, arithmetic and copies ran while one was open for 23% of the time, Pallas kernels for 0%

commit v1 on v0

--- a/solution.py
+++ b/solution.py
@@ -89,7 +89,9 @@
     qkv = jnp.dot(h_one, full_qkv, preferred_element_type=jnp.float32)
     q_heads = qkv[:, :width].astype(jnp.bfloat16).reshape(wins, blocks_dev, BLK, H, HD)
     keyval = qkv[:, width:].astype(jnp.bfloat16).reshape(wins, local_len, 2 * width)
-    window = lax.all_gather(keyval, "seq", axis=1, tiled=True)
+    window = jnp.concatenate(
+        lax.all_to_all(jnp.stack([keyval] * lax.axis_size("seq")), "seq", 0, 0), axis=1
+    )
     shaped = window.reshape(wins, block_count * BLK, 2, H, HD)
     keys, values = (shaped[:, :, 0], shaped[:, :, 1])
     scores = (

time: 690 us -> 706 us (1.023)
  local copies, waits for them, and re-layouts: 69 us -> 91.4 us
  waiting for transfers between devices: 286 us -> 275 us
    all_to_all x0 -> x1, waiting for transfers between devices: none -> 60.4 us  [per_device(): lax.all_to_all(jnp.stack([keyval] * lax.axis_size('seq')), 'seq', 0, 0)]
    all_gather x4, waiting for transfers between devices: 45.8 us -> 0.08 us  [per_device(): lax.all_gather(lax.all_gather(low, 'win', axis=1, tiled=True), 'seq', axi...]
    all_gather x1 -> x0, waiting for transfers between devices: 23.8 us -> none  [per_device(): window = lax.all_gather(keyval, 'seq', axis=1, tiled=True)]
    another operation x0 -> x3, local copies, waits for them, and re-layouts: none -> 14.6 us  [the longest x1 10.3 us: per_device(): shaped = window.reshape(wins, block_count * BLK, 2, H, HD)]
    reshape x1, local copies, waits for them, and re-layouts: 1.15 us -> 8.67 us  [per_device(): jnp.concatenate(lax.all_to_all(jnp.stack([keyval] * lax.axis_size('seq'))...]
    unnamed x89 -> x91, local copies, waits for them, and re-layouts: 52.3 us -> 52.6 us
    unnamed x18 -> x17, waiting for transfers between devices: 78.1 us -> 78.1 us
  transfers between devices with their start and end apart: 14 -> 14, of which waited for: 10 -> 8; matrix products, arithmetic and copies ran while one was open for 23% -> 25% of each run, Pallas kernels for 0% -> 0%
where the time goes in v1:
time: 706 us; the launch traced here: 698 us
  waiting for transfers between devices  275 us (39%)
  blocking collectives  186 us (26%)
  local copies, waits for them, and re-layouts  91.4 us (13%)
  matrix products  79.2 us (11%)
  other arithmetic  40.6 us (6%)
  between operations  20 us (3%)
    reduce_scatter x4, waiting for transfers between devices, per_device(): lax.psum_scatter(raw.astype(jnp.bfloat16), 'seq', scatter_dimension=0, ti...  115 us
    unnamed x2, blocking collectives  79 us
    unnamed x17, waiting for transfers between devices  78.1 us
    all_gather x4, blocking collectives, per_device(): lax.all_gather(low, 'win', axis=1, tiled=True)  65.8 us
    all_to_all x1, waiting for transfers between devices, per_device(): lax.all_to_all(jnp.stack([keyval] * lax.axis_size('seq')), 'seq', 0, 0)  60.4 us
    unnamed x91, local copies, waits for them, and re-layouts  52.6 us
    psum x1, blocking collectives, per_device(): grad_norm = jnp.sqrt(lax.psum(local_squares, ('win', 'seq')))  40.9 us
    reduce_scatter x1, waiting for transfers between devices, per_device(): lax.psum_scatter(lax.psum_scatter(raw.astype(jnp.bfloat16), 'seq', scatte...  21.6 us
  transfers between devices with their start and end apart: 14, of which 8 were waited for; matrix products, arithmetic and copies ran while one was open for 25% of the time, Pallas kernels for 0%

profile of v1, /device:TPU:0, one launch (start us, length us, event | category | flops | bytes accessed | tf_op | source)
XLA Modules:
  0.0 697.8 jit_solution(12916912149934830340)
XLA Ops:
  8.3 17.0 %all-gather = bf16[4,576,96]{1,2,0:T(8,128)(2,1)S(1)} all-gather(bf16[1,576,96]{1,2,0:T(8,128)(2,1)S(1)} %convert_bitcast_fusion), channel_id=1, replica_groups=mesh['win'=4,'seq'=8] {'win'}, dimensions={0}, use_global_device_ids=true | all-gather | bytes 552960 | tf_op jit(solution)/shard_map/all_gather | solution.py:78
  26.8 17.8 %all_gather.34 = bf16[384,768]{0,1:T(8,128)(2,1)} all-gather(bf16[384,192]{0,1:T(8,128)(2,1)S(1)} %convert_element_type.148), channel_id=1, replica_groups=mesh['win'=4,'seq'=8] {'win'}, dimensions={1}, use_global_device_ids=true | all-gather | bytes 737280 | tf_op jit(solution)/shard_map/all_gather | solution.py:78
  44.8 13.6 %all_gather.30 = bf16[96,768]{0,1:T(8,128)(2,1)S(1)} all-gather(bf16[96,192]{0,1:T(8,128)(2,1)S(1)} %copy.164), channel_id=1, replica_groups=mesh['win'=4,'seq'=8] {'win'}, dimensions={1}, use_global_device_ids=true | all-gather | bytes 184320 | tf_op jit(solution)/shard_map/all_gather | solution.py:78
  59.9 39.5 %all-reduce = bf16[3072]{0:T(1024)(128)(2,1)S(1)} all-reduce(bf16[3072]{0:T(1024)(128)(2,1)S(1)} %dynamic-update-slice), channel_id=1, replica_groups=mesh['win'=4,'seq'=8] {'win','seq'}, use_global_device_ids=true, to_apply=%add | all-reduce | flops 3072 | bytes 12288
  99.7 3.2 convolution_convert_fusion.3
  104.3 3.9 stack.15
  108.2 4.9 all-to-all-start
  113.2 17.5 %all_gather.32 = bf16[96,3072]{1,0:T(8,128)(2,1)} all-gather(bf16[96,768]{1,0:T(8,128)(2,1)S(1)} %convert_element_type.146), channel_id=1, replica_groups=mesh['win'=4,'seq'=8] {'win'}, dimensions={1}, use_global_device_ids=true | all-gather | bytes 737280 | tf_op jit(solution)/shard_map/all_gather | solution.py:78
  133.5 5.4 fusion.66
  138.9 60.4 %all-to-all-done = bf16[8,2,128,1536]{2,3,1,0:T(8,128)(2,1)} async-done(((bf16[8,2,128,1536]{2,3,1,0:T(8,128)(2,1)}), bf16[8,2,128,1536]{2,3,1,0:T(8,128)(2,1)}, u32[]{:S(2)}, u32[]{:S(2)}) %all-to-all-start) | async-done | bytes 6291488 | tf_op jit(solution)/shard_map/all_to_all | solution.py:93
  199.3 8.7 %copy.157 = bf16[2,8,128,1536]{2,1,3,0:T(8,128)(2,1)} copy(bf16[2,8,128,1536]{2,3,0,1:T(8,128)(2,1)} %bitcast.7) | data formatting | bytes 12582912 | tf_op jit(solution)/shard_map/reshape | solution.py:92
  208.0 10.3 %reshape_reshape.3 = bf16[2,1024,2,12,64]{1,4,3,2,0:T(8,128)(2,1)} reshape(bf16[2,8,128,1536]{2,1,3,0:T(8,128)(2,1)} %copy.157) | data formatting | bytes 12582912 | tf_op jit(solution)/shard_map/reshape;reshape | solution.py:95
  218.3 3.7 fusion.17
  223.3 3.0 exponential_reduce_fusion
  226.6 2.4 exponential_convert_fusion
  229.0 7.3 %fusion.30 = bf16[2,2,64,12,64]{2,4,1,3,0:T(8,128)(2,1)S(1)} fusion(bf16[2,2,12,64,1024]{4,3,1,2,0:T(8,128)(2,1)S(1)} %exponential_convert_fusion, bf16[2,1024,2,12,64]{1,4,3,2,0:T(8,128)(2,1)} %reshape_reshape.3), kind=kOutput, calls=%fused_computation.43 | convolution fusion | flops 402849792 | bytes 9830400 | tf_op jit(solution)/shard_map/wbhqk,wkhd->wbqhd/dot_general | solution.py:105
  237.6 1.9 fusion.65
  239.7 8.0 %fusion.10 = (bf16[256,3072]{1,0:T(8,128)(2,1)S(1)}, f32[256,3072]{1,0:T(8,128)}) fusion(f32[256,3072]{1,0:T(8,128)} %fusion.66, bf16[768,3072]{1,0:T(8,128)(2,1)} %all-gather.10.cloned.1.call-done, f32[256,768]{1,0:T(8,128)S(1)} %get-tuple-element.196, f32[768]{0:T(1024)S(1)} %get-tuple-element.190, f32[768]{0:T(1024)S(1)} %get-tuple-element.189, ...), kind=kOutput, calls=%fused_computation.24 | convolution fusion | flops 1224671232 | bytes 13377536 | tf_op jit(solution)/shard_map/dot_general | solution.py:109
  251.5 6.3 convolution_convert_fusion
  257.8 5.2 convolution_convert_fusion.1
  268.5 6.0 fusion.12
  274.5 6.3 fusion.13
  280.7 7.8 %fusion = f32[2,2,12,64]{3,1,2,0:T(2,128)S(1)} fusion(f32[2,2,12,64,1024]{4,3,1,2,0:T(8,128)} %bitcast.169, bf16[2,2,12,64,1024]{4,3,1,2,0:T(8,128)(2,1)} %copy-done.1), kind=kLoop, calls=%fused_computation.2 | loop fusion | flops 9434112 | bytes 18886656 | tf_op jit(solution)/shard_map/reduce_sum | solution.py:130
  288.6 10.0 %fusion.1 = bf16[2,2,12,64,1024]{4,3,1,2,0:T(8,128)(2,1)S(1)} fusion(f32[2,2,12,64]{3,1,2,0:T(2,128)S(1)} %fusion, f32[2,12,1024,128]{2,3,1,0} %fusion.13, f32[2,2,12,64]{3,1,2,0:T(2,128)S(1)} %bitcast.188, f32[2,2,12,1024]{3,1,2,0:T(2,128)S(1)} %copy-done.8, f32[2,12,1024,128]{2,3,1,0} %copy-done), kind=kLoop, calls=%fused_computation.3 | loop fusion | flops 25165824 | bytes 31678464 | tf_op jit(solution)/shard_map/convert_element_type | solution.py:131
  298.6 2.9 copy-done.2
  304.3 3.4 copy.171
  307.6 16.6 %copy.187 = bf16[2,1024,1536]{2,0,1:T(2,128)(2,1)} copy(bf16[2,1024,1536]{1,2,0:T(8,128)(2,1)} %bitcast.171) | data formatting | bytes 12582912
  324.2 7.1 %copy.203 = bf16[128,8,2,1536]{3,1,2,0:T(8,128)(2,1)} copy(bf16[128,8,2,1536]{3,2,1,0:T(2,128)(2,1)} %bitcast.172) | data formatting | bytes 12582912
  333.2 11.4 %reduce-scatter.26.cloned.1.call-done = bf16[384,768]{1,0:T(8,128)(2,1)} async-done(((bf16[3072,768]{1,0:T(8,128)(2,1)}), bf16[384,768]{1,0:T(8,128)(2,1)}) %reduce-scatter.26.cloned.1.call-update) | async-done | bytes 589840 | tf_op jit(solution)/shard_map/reduce_scatter | solution.py:153
  344.6 2.1 copy.193
  346.9 55.2 %reduce-scatter.22.cloned.1.call-done = bf16[96,3072]{1,0:T(8,128)(2,1)} async-done(((bf16[768,3072]{1,0:T(8,128)(2,1)}), bf16[96,3072]{1,0:T(8,128)(2,1)}) %reduce-scatter.22.cloned.1.call-update) | async-done | bytes 589840 | tf_op jit(solution)/shard_map/reduce_scatter | solution.py:153
  402.3 6.9 fusion.33
  410.8 2.6 reshape.261
  413.4 54.1 %reduce-scatter.28.cloned.1.call-done = bf16[128,3072]{1,0:T(8,128)(2,1)} async-done(((bf16[1024,3072]{1,0:T(8,128)(2,1)}), bf16[128,3072]{1,0:T(8,128)(2,1)}) %reduce-scatter.28.cloned.1.call-update) | async-done | bytes 786448
  467.5 3.2 reshape.263
  472.0 3.9 convolution_convert_fusion.2
  477.1 1.9 copy.174
  479.0 1.9 copy.175
  480.9 6.1 fusion.36
  486.9 2.8 reduce-scatter.32.cloned.1.call-done
  491.3 20.9 %reduce-scatter.34.cloned.1.call-done = bf16[192,384]{1,0:T(8,128)(2,1)} async-done(((bf16[768,384]{1,0:T(8,128)(2,1)}), bf16[192,384]{1,0:T(8,128)(2,1)}) %reduce-scatter.34.cloned.1.call-update) | async-done | bytes 147472
  513.2 21.6 %reduce-scatter.24.cloned.1.call-done = bf16[96,768]{1,0:T(8,128)(2,1)} async-done(((bf16[96,3072]{1,0:T(8,128)(2,1)}), bf16[96,768]{1,0:T(8,128)(2,1)}) %reduce-scatter.24.cloned.1.call-update) | async-done | bytes 147472 | tf_op jit(solution)/shard_map/reduce_scatter | solution.py:152
  537.1 48.0 %reduce-scatter.18.cloned.1.call-done = bf16[96,2304]{1,0:T(8,128)(2,1)} async-done(((bf16[768,2304]{1,0:T(8,128)(2,1)}), bf16[96,2304]{1,0:T(8,128)(2,1)}) %reduce-scatter.18.cloned.1.call-update) | async-done | bytes 442384 | tf_op jit(solution)/shard_map/reduce_scatter | solution.py:153
  585.1 2.1 copy.189
  587.2 3.3 multiply_reduce_fusion.2
  591.1 39.5 %all-reduce.1 = f32[3072]{0:T(1024)S(1)} all-reduce(f32[3072]{0:T(1024)S(1)} %pad_maximum_fusion.4), channel_id=11, replica_groups=mesh['win'=4,'seq'=8] {'win','seq'}, use_global_device_ids=true, to_apply=%region_29.30.clone | all-reduce | flops 3072 | bytes 24576
  639.0 40.9 %psum.7 = f32[]{:T(128)} all-reduce(f32[]{:T(128)S(6)} %add.254), channel_id=1, replica_groups=mesh['win'=4,'seq'=8] {'win','seq'}, use_global_device_ids=true, to_apply=%region_31.32 | all-reduce | flops 1 | bytes 8 | tf_op jit(solution)/shard_map/psum | solution.py:165
  686.8 2.1 multiply_subtract_fusion.2
  (178 shorter events, 47.7 us)
Async XLA Ops:
  7.2 19.6 %copy-start.17 = (f32[384,192]{0,1:T(8,128)S(1)}, f32[384,192]{0,1:T(8,128)}, u32[]{:S(2)}) copy-start(f32[384,192]{0,1:T(8,128)} %param.26) | copy-start | bytes 884740
  7.2 37.5 %copy-start.21 = (f32[96,192]{1,0:T(8,128)S(1)}, f32[96,192]{1,0:T(8,128)}, u32[]{:S(2)}) copy-start(f32[96,192]{1,0:T(8,128)} %param.24) | copy-start | bytes 221188
  7.2 52.0 %copy-start.28 = (f32[96]{0:T(128)S(1)}, f32[96]{0:T(128)}, u32[]{:S(2)}) copy-start(f32[96]{0:T(128)} %param.27) | copy-start | bytes 1156
  7.2 52.0 %copy-start.3 = (bf16[2,128,768]{2,1,0:T(8,128)(2,1)S(1)}, bf16[2,128,768]{2,1,0:T(8,128)(2,1)}, u32[]{:S(2)}) copy-start(bf16[2,128,768]{2,1,0:T(8,128)(2,1)} %param.19) | copy-start | bytes 1179652
  7.2 92.4 %all-gather.6.cloned.1.call-start = ((), (), s32[]{:S(2)}) async-start(), calls=%async_computation.10 | async-start | bytes 3981312 | tf_op jit(solution)/shard_map/all_gather | solution.py:78
  26.8 106.8 %all-gather.12.cloned.1.call-start = ((), (), s32[]{:S(2)}) async-start(), calls=%async_computation.13 | async-start | bytes 5308416 | tf_op jit(solution)/shard_map/all_gather | solution.py:78
  44.6 193.0 %all-gather.8.cloned.1.call-start = ((), (), s32[]{:S(2)}) async-start(), calls=%async_computation.11 | async-start | bytes 1327104 | tf_op jit(solution)/shard_map/all_gather | solution.py:78
  99.6 3.3 copy-start.9
  108.2 5.0 copy-start.15
  108.2 22.6 %copy-start.32 = (s32[2]{0:T(128)S(1)}, s32[2]{0:T(128)}, u32[]{:S(2)}) copy-start(s32[2]{0:T(128)} %param.22) | copy-start | bytes 28
  108.2 22.6 %copy-start.27 = (s32[2,2,12,3]{2,1,3,0:T(2,128)S(1)}, s32[2,2,12,3]{2,1,3,0:T(2,128)}, u32[]{:S(2)}) copy-start(s32[2,2,12,3]{2,1,3,0:T(2,128)} %param.21) | copy-start | bytes 1732
  108.2 91.1 %all-to-all-start = ((bf16[8,2,128,1536]{2,3,1,0:T(8,128)(2,1)}), bf16[8,2,128,1536]{2,3,1,0:T(8,128)(2,1)}, u32[]{:S(2)}, u32[]{:S(2)}) async-start(bf16[8,2,128,1536]{2,3,1,0:T(8,128)(2,1)} %stack.15), calls=%async_computation | async-start | bytes 12582912 | tf_op jit(solution)/shard_map/all_to_all | solution.py:93
  113.1 18.5 %copy-start.23 = (bf16[2,128,768]{2,1,0:T(8,128)(2,1)S(1)}, bf16[2,128,768]{2,1,0:T(8,128)(2,1)}, u32[]{:S(2)}) copy-start(bf16[2,128,768]{2,1,0:T(8,128)(2,1)} %param.20) | copy-start | bytes 1179652
  113.1 19.6 %slice-start.2 = ((bf16[256,2304]{1,0:T(8,128)(2,1)}), bf16[256,768]{1,0:T(8,128)(2,1)S(1)}, s32[]{:S(2)}) async-start(bf16[256,2304]{1,0:T(8,128)(2,1)} %copy-done.13), calls=%async_computation.25 | async-start | bytes 786432 | tf_op jit(solution)/shard_map/slice | solution.py:90
  113.1 126.6 %all-gather.10.cloned.1.call-start = ((), (), s32[]{:S(2)}) async-start(), calls=%async_computation.12 | async-start | bytes 5308416 | tf_op jit(solution)/shard_map/all_gather | solution.py:78
  130.7 200.7 %reduce-scatter.20.cloned.1.call-start = ((), (), s32[]{:S(2)}) async-start(), calls=%async_computation.15 | async-start | bytes 1327104 | tf_op jit(solution)/shard_map/reduce_scatter | solution.py:153
  131.6 94.7 %copy-start.7 = (f32[2,2,12,1024]{3,1,2,0:T(2,128)}, f32[2,2,12,1024]{3,1,2,0:T(2,128)S(1)}, u32[]{:S(2)}) copy-start(f32[2,2,12,1024]{3,1,2,0:T(2,128)S(1)} %add.238) | copy-start | bytes 589828
  132.7 6.2 copy-start.24
  222.0 4.6 copy-start
  229.0 7.3 %copy-start.1 = (bf16[2,2,12,64,1024]{4,3,1,2,0:T(8,128)(2,1)}, bf16[2,2,12,64,1024]{4,3,1,2,0:T(8,128)(2,1)S(1)}, u32[]{:S(2)}) copy-start(bf16[2,2,12,64,1024]{4,3,1,2,0:T(8,128)(2,1)S(1)} %exponential_convert_fusion) | copy-start | bytes 18874372
  239.7 8.0 %copy-start.31 = (bf16[768,3072]{1,0:T(8,128)(2,1)S(1)}, bf16[768,3072]{1,0:T(8,128)(2,1)}, u32[]{:S(2)}) copy-start(bf16[768,3072]{1,0:T(8,128)(2,1)} %all-gather.10.cloned.1.call-done) | copy-start | bytes 14155780
  247.7 1.6 copy-start.14
  247.7 2.0 copy-start.6
  251.4 93.2 %reduce-scatter.26.cloned.1.call-start = ((), (), s32[]{:S(2)}) async-start(), calls=%async_computation.18 | async-start | bytes 5308416 | tf_op jit(solution)/shard_map/reduce_scatter | solution.py:153
  257.8 144.3 %reduce-scatter.22.cloned.1.call-start = ((), (), s32[]{:S(2)}) async-start(), calls=%async_computation.16 | async-start | bytes 5308416 | tf_op jit(solution)/shard_map/reduce_scatter | solution.py:153
  263.1 204.5 %reduce-scatter.28.cloned.1.call-start = ((), (), s32[]{:S(2)}) async-start(), calls=%async_computation.19 | async-start | bytes 7077888
  266.9 7.6 %slice-start = ((s8[6291456]{0:T(1024)(128)(4,1)}), s8[4194304]{0:T(1024)(128)(4,1)S(1)}, s32[]{:S(2)}) async-start(s8[6291456]{0:T(1024)(128)(4,1)} %bitcast.173), calls=%async_computation.23 | async-start | bytes 8388608
  268.5 6.0 slice-start.1
  280.7 7.8 %copy-start.8 = (f32[2,2,12,1024]{3,1,2,0:T(2,128)S(1)}, f32[2,2,12,1024]{3,1,2,0:T(2,128)}, u32[]{:S(2)}) copy-start(f32[2,2,12,1024]{3,1,2,0:T(2,128)} %copy-done.7) | copy-start | bytes 589828
  298.6 2.9 copy-start.2
  301.5 2.2 copy-start.4
  331.3 158.4 %reduce-scatter.32.cloned.1.call-start = ((), (), s32[]{:S(2)}) async-start(), calls=%async_computation.21 | async-start | bytes 245760
  333.2 179.0 %reduce-scatter.34.cloned.1.call-start = ((), (), s32[]{:S(2)}) async-start(), calls=%async_computation.22 | async-start | bytes 737280
  346.8 188.0 %reduce-scatter.24.cloned.1.call-start = ((), (), s32[]{:S(2)}) async-start(), calls=%async_computation.17 | async-start | bytes 737280 | tf_op jit(solution)/shard_map/reduce_scatter | solution.py:152
  402.1 183.1 %reduce-scatter.18.cloned.1.call-start = ((), (), s32[]{:S(2)}) async-start(), calls=%async_computation.14 | async-start | bytes 3981312 | tf_op jit(solution)/shard_map/reduce_scatter | solution.py:153
  409.1 62.9 %copy-start.10 = (bf16[256,768]{1,0:T(8,128)(2,1)S(1)}, bf16[256,768]{1,0:T(8,128)(2,1)}, u32[]{:S(2)}) copy-start(bf16[256,768]{1,0:T(8,128)(2,1)} %copy-done.9) | copy-start | bytes 1179652
  475.9 155.4 %reduce-scatter.30.cloned.1.call-start = ((), (), s32[]{:S(2)}) async-start(), calls=%async_computation.20 | async-start | bytes 737280
  590.6 90.0 %copy-start.11 = (f32[384,192]{1,0:T(8,128)S(1)}, f32[384,192]{1,0:T(8,128)}, u32[]{:S(2)}) copy-start(f32[384,192]{1,0:T(8,128)} %copy.174) | copy-start | bytes 884740
  590.6 90.0 %copy-start.12 = (f32[384,192]{1,0:T(8,128)S(1)}, f32[384,192]{1,0:T(8,128)}, u32[]{:S(2)}) copy-start(f32[384,192]{1,0:T(8,128)} %copy.175) | copy-start | bytes 884740
  639.0 45.5 %copy-start.29 = (f32[96]{0:T(128)S(1)}, f32[96]{0:T(128)}, u32[]{:S(2)}) copy-start(f32[96]{0:T(128)} %param.37) | copy-start | bytes 1156
  639.0 45.5 %copy-start.30 = (f32[96]{0:T(128)S(1)}, f32[96]{0:T(128)}, u32[]{:S(2)}) copy-start(f32[96]{0:T(128)} %param.32) | copy-start | bytes 1156
  639.0 46.1 %copy-start.22 = (f32[96,192]{1,0:T(8,128)S(1)}, f32[96,192]{1,0:T(8,128)}, u32[]{:S(2)}) copy-start(f32[96,192]{1,0:T(8,128)} %param.24) | copy-start | bytes 221188
  680.6 6.2 copy-start.18
  680.6 6.2 copy-start.19
  680.9 7.9 %copy-start.16 = (f32[96,768]{1,0:T(8,128)S(1)}, f32[96,768]{1,0:T(8,128)}, u32[]{:S(2)}) copy-start(f32[96,768]{1,0:T(8,128)} %param.25) | copy-start | bytes 884740
  681.0 7.9 %copy-start.20 = (bf16[96,768]{1,0:T(8,128)(2,1)S(1)}, bf16[96,768]{1,0:T(8,128)(2,1)}, u32[]{:S(2)}) copy-start(bf16[96,768]{1,0:T(8,128)(2,1)} %reduce-scatter.24.cloned.1.call-done) | copy-start | bytes 442372
  681.0 7.9 %copy-start.25 = (f32[96,768]{1,0:T(8,128)S(1)}, f32[96,768]{1,0:T(8,128)}, u32[]{:S(2)}) copy-start(f32[96,768]{1,0:T(8,128)} %param.35) | copy-start | bytes 884740
  681.0 7.9 %copy-start.26 = (f32[96,768]{1,0:T(8,128)S(1)}, f32[96,768]{1,0:T(8,128)}, u32[]{:S(2)}) copy-start(f32[96,768]{1,0:T(8,128)} %param.30) | copy-start | bytes 884740
  (2 other events, 1.9 us)
Sparse Core Ops, SparseCore 0:
  26.9 35.7 all-gather.5
  64.5 40.3 all-gather.11
  107.4 53.0 all-gather.7
  162.2 47.7 all-gather.9
  251.5 35.4 reduce-scatter.19
  290.7 53.8 reduce-scatter.25
  348.1 53.8 reduce-scatter.21
  405.8 61.7 reduce-scatter.27
  470.4 19.3 reduce-scatter.31
  492.0 20.1 reduce-scatter.33
  514.6 20.2 reduce-scatter.23
  538.6 46.5 reduce-scatter.17
  588.1 21.8 reduce-scatter.29
